TPU v7x, 32 devices: a whole 2x2x4 slice. The times are simulated.
32 devices in a mesh: rows: 4 (over y, x), cols: 8 (over z, core).
Axes of the slice: x: 2, y: 2, z: 4, core: 2. Of those that a mesh axis runs over, the one named last changes fastest.
Arguments:
- tokens: bfloat16 [128, 256, 256], P('rows', 'cols'), may hold values from -45 to 45
- key_bias: bfloat16 [128, 256], P('rows', 'cols'), may hold values from -3 to 250
- cotangent: bfloat16 [128, 256, 256], P('rows', 'cols'), may hold values from -6 to 6
- gain_row: float32 [256], replicated, may hold values from 0.1 to 1.9
- w_qkv_row: bfloat16 [256, 768], replicated, may hold values from -0.375 to 0.375
- w_out_row: bfloat16 [256, 256], replicated, may hold values from -0.375 to 0.375
- gain_col: float32 [256], replicated, may hold values from 0.1 to 1.9
- w_qkv_col: bfloat16 [256, 768], replicated, may hold values from -0.375 to 0.375
- w_out_col: bfloat16 [256, 256], replicated, may hold values from -0.375 to 0.375
- gain_mlp: float32 [256], replicated, may hold values from 0.1 to 1.9
- w_up: bfloat16 [256, 1024], replicated, may hold values from -0.375 to 0.375
- w_down: bfloat16 [1024, 256], replicated, may hold values from -0.1875 to 0.1875
Outputs:
- d_tokens: bfloat16 [128, 256, 256], P('rows', 'cols')
- d_gain_row: float32 [256], replicated
- d_w_qkv_row: float32 [256, 768], replicated
- d_w_out_row: float32 [256, 256], replicated
- d_gain_col: float32 [256], replicated
- d_w_qkv_col: float32 [256, 768], replicated
- d_w_out_col: float32 [256, 256], replicated
- d_gain_mlp: float32 [256], replicated
- d_w_up: float32 [256, 1024], replicated
- d_w_down: float32 [1024, 256], replicated
All inputs are finite; a program needn't handle non-finite values.
Results may differ from a plain program's by a relative error of at most 0.015.
Values may be sent and summed in bfloat16 or wider, within the bound.
No kernel may reach another device: no remote copies, remote signals or barrier semaphores. Data moves between devices by JAX's collectives and lax.ppermute only.
A program may use at most 128 MiB of HBM per device.

v0:
```python
import jax
import jax.numpy as jnp
from jax import lax
from jax.sharding import PartitionSpec as P

HEADS = 4


def product(spec_text, left_op, right_op):
    return jnp.einsum(spec_text, left_op, right_op, preferred_element_type=jnp.float32)


def layer_norm(entries, gain_vec):
    floats = entries.astype(jnp.float32)
    centred = floats - jnp.mean(floats, axis=-1, keepdims=True)
    inverse = lax.rsqrt(jnp.mean(centred * centred, axis=-1, keepdims=True) + 1e-05)
    normed = centred * inverse
    return ((normed * gain_vec).astype(jnp.bfloat16), normed, inverse)


def norm_back(grad_out, normed, inverse, gain_vec):
    scaled = grad_out * gain_vec
    result = inverse * (
        scaled
        - jnp.mean(scaled, axis=-1, keepdims=True)
        - normed * jnp.mean(scaled * normed, axis=-1, keepdims=True)
    )
    gain_grad = jnp.sum((grad_out * normed).reshape(-1, gain_vec.shape[0]), axis=0)
    return (result, gain_grad)


def over_cells(left_op, right_op):
    left_flat = left_op.reshape(-1, left_op.shape[-1])
    right_flat = right_op.reshape(-1, right_op.shape[-1])
    return lax.dot_general(
        left_flat, right_flat, (((0,), (0,)), ((), ())), preferred_element_type=jnp.float32
    )


def times_transpose(entries, weight):
    return lax.dot_general(
        entries, weight, (((entries.ndim - 1,), (1,)), ((), ())), preferred_element_type=jnp.float32
    )


def letters(length_axis):
    if length_axis == 1:
        return ("sqhd,skhd->shqk", "shqk,skhd->sqhd", "shqk,sqhd->skhd")
    return ("qshd,kshd->shqk", "shqk,kshd->qshd", "shqk,qshd->kshd")


def split_heads(packed, head_count):
    features = packed.shape[-1] // 3
    head_shape = packed.shape[:-1] + (head_count, features // head_count)
    return tuple(
        (
            packed[..., member * features : (member + 1) * features].reshape(head_shape)
            for member in range(3)
        )
    )


def key_terms(bias_rows, length_axis):
    floats = bias_rows.astype(jnp.float32)
    if length_axis == 0:
        floats = floats.T
    return floats[:, None, None, :]


def attention_weights(query_block, key_rows, bias_terms, factor, length_axis):
    scores = product(letters(length_axis)[0], query_block, key_rows) * factor + bias_terms
    shifted = jnp.exp(scores - jnp.max(scores, axis=-1, keepdims=True))
    return shifted / jnp.sum(shifted, axis=-1, keepdims=True)


def join_blocks(stacked, length_axis, features):
    if length_axis == 0:
        return stacked.reshape((-1, stacked.shape[2], features))
    reordered = jnp.moveaxis(stacked, 0, 1)
    return reordered.reshape((reordered.shape[0], -1, features))


def attend(packed, bias_rows, head_count, length_axis):
    query_rows, key_rows, value_rows = split_heads(packed, head_count)
    length = packed.shape[length_axis]
    block_len = min(length, 512)
    factor = query_rows.shape[-1] ** (-0.5)
    bias_terms = key_terms(bias_rows, length_axis)
    mixing = letters(length_axis)[1]

    def one_block(offset):
        query_block = lax.dynamic_slice_in_dim(query_rows, offset, block_len, length_axis)
        weights = attention_weights(query_block, key_rows, bias_terms, factor, length_axis)
        return product(mixing, weights.astype(jnp.bfloat16), value_rows).astype(jnp.bfloat16)

    offsets = jnp.arange(length // block_len, dtype=jnp.int32) * block_len
    return join_blocks(lax.map(one_block, offsets), length_axis, packed.shape[-1] // 3)


def attend_back(grad_out, packed, bias_rows, head_count, length_axis):
    query_rows, key_rows, value_rows = split_heads(packed, head_count)
    features = packed.shape[-1] // 3
    grad_heads = grad_out.reshape(query_rows.shape)
    length = packed.shape[length_axis]
    block_len = min(length, 512)
    factor = query_rows.shape[-1] ** (-0.5)
    bias_terms = key_terms(bias_rows, length_axis)
    score_spec, mixing, gather_spec = letters(length_axis)

    def one_block(running, offset):
        key_grad, value_grad = running
        query_block = lax.dynamic_slice_in_dim(query_rows, offset, block_len, length_axis)
        grad_block = lax.dynamic_slice_in_dim(grad_heads, offset, block_len, length_axis)
        weights = attention_weights(query_block, key_rows, bias_terms, factor, length_axis)
        weights_low = weights.astype(jnp.bfloat16)
        weight_grad = product(score_spec, grad_block, value_rows)
        centre = jnp.sum(weights * weight_grad, axis=-1, keepdims=True)
        score_grad = (weights * (weight_grad - centre) * factor).astype(jnp.bfloat16)
        query_grad = product(mixing, score_grad, key_rows)
        key_grad = key_grad + product(gather_spec, score_grad, query_block)
        value_grad = value_grad + product(gather_spec, weights_low, grad_block)
        return ((key_grad, value_grad), query_grad)

    empty_grad = jnp.zeros(key_rows.shape, jnp.float32)
    offsets = jnp.arange(length // block_len, dtype=jnp.int32) * block_len
    (key_grad, value_grad), query_parts = lax.scan(one_block, (empty_grad, empty_grad), offsets)
    query_grad = join_blocks(query_parts, length_axis, features)
    flat_shape = packed.shape[:-1] + (features,)
    joined = jnp.concatenate(
        [query_grad, key_grad.reshape(flat_shape), value_grad.reshape(flat_shape)], axis=-1
    )
    return joined.astype(jnp.bfloat16)


def attention_forward(inputs, bias_rows, gain_vec, w_qkv, w_out, head_count, length_axis):
    normal_in, normed, inverse = layer_norm(inputs, gain_vec)
    packed = jnp.dot(normal_in, w_qkv, preferred_element_type=jnp.float32).astype(jnp.bfloat16)
    mixed_out = attend(packed, bias_rows, head_count, length_axis)
    output = (
        inputs.astype(jnp.float32) + jnp.dot(mixed_out, w_out, preferred_element_type=jnp.float32)
    ).astype(jnp.bfloat16)
    return (output, (normal_in, normed, inverse, packed, mixed_out))


def attention_backward(
    grad_out, saved_parts, bias_rows, gain_vec, w_qkv, w_out, head_count, length_axis
):
    normal_in, normed, inverse, packed, mixed_out = saved_parts
    out_grad = over_cells(mixed_out, grad_out)
    mixed_grad = times_transpose(grad_out, w_out).astype(jnp.bfloat16)
    packed_grad = attend_back(mixed_grad, packed, bias_rows, head_count, length_axis)
    qkv_grad = over_cells(normal_in, packed_grad)
    input_grad, gain_grad = norm_back(
        times_transpose(packed_grad, w_qkv), normed, inverse, gain_vec
    )
    return (
        (grad_out.astype(jnp.float32) + input_grad).astype(jnp.bfloat16),
        (gain_grad, qkv_grad, out_grad),
    )


def feed_backward(inputs, grad_out, gain_vec, w_up, w_down):
    normal_in, normed, inverse = layer_norm(inputs, gain_vec)
    hidden = jnp.dot(normal_in, w_up, preferred_element_type=jnp.float32)
    active, gelu_back = jax.vjp(jax.nn.gelu, hidden)
    active_low = active.astype(jnp.bfloat16)
    down_grad = over_cells(active_low, grad_out)
    hidden_grad = gelu_back(times_transpose(grad_out, w_down))[0].astype(jnp.bfloat16)
    up_grad = over_cells(normal_in, hidden_grad)
    input_grad, gain_grad = norm_back(times_transpose(hidden_grad, w_up), normed, inverse, gain_vec)
    return (
        (grad_out.astype(jnp.float32) + input_grad).astype(jnp.bfloat16),
        (gain_grad, up_grad, down_grad),
    )


def shards(
    tokens,
    key_bias,
    cotangent,
    gain_row,
    w_qkv_row,
    w_out_row,
    gain_col,
    w_qkv_col,
    w_out_col,
    gain_mlp,
    w_up,
    w_down,
):
    row_cells, row_bias = (
        lax.all_to_all(tokens, "cols", split_axis=0, concat_axis=1, tiled=True),
        lax.all_to_all(key_bias, "cols", split_axis=0, concat_axis=1, tiled=True),
    )
    after_rows, row_saved = attention_forward(
        row_cells, row_bias, gain_row, w_qkv_row, w_out_row, HEADS, 1
    )
    column_cells = lax.all_to_all(
        lax.all_to_all(after_rows, "cols", split_axis=1, concat_axis=0, tiled=True),
        "rows",
        split_axis=1,
        concat_axis=0,
        tiled=True,
    )
    column_grads, column_bias = (
        lax.all_to_all(cotangent, "rows", split_axis=1, concat_axis=0, tiled=True),
        lax.all_to_all(key_bias, "rows", split_axis=1, concat_axis=0, tiled=True),
    )
    after_cols, column_saved = attention_forward(
        column_cells, column_bias, gain_col, w_qkv_col, w_out_col, HEADS, 0
    )
    mid_grad, feed_grads = feed_backward(after_cols, column_grads, gain_mlp, w_up, w_down)
    cell_grad, attn_grads = attention_backward(
        mid_grad, column_saved, column_bias, gain_col, w_qkv_col, w_out_col, HEADS, 0
    )
    factor = float(
        tokens.shape[0] * tokens.shape[1] * lax.axis_size("rows") * lax.axis_size("cols")
    ) ** (-0.5)
    other_sums = tuple((grad_term * factor for grad_term in attn_grads + feed_grads))
    grad_rows = lax.all_to_all(
        lax.all_to_all(cell_grad, "rows", split_axis=0, concat_axis=1, tiled=True),
        "cols",
        split_axis=0,
        concat_axis=1,
        tiled=True,
    )
    token_grad_rows, row_grads = attention_backward(
        grad_rows, row_saved, row_bias, gain_row, w_qkv_row, w_out_row, HEADS, 1
    )
    d_tokens = lax.all_to_all(token_grad_rows, "cols", split_axis=1, concat_axis=0, tiled=True)
    row_sums = tuple((grad_term * factor for grad_term in row_grads))
    summed = lax.psum(
        (
            row_sums[0],
            row_sums[1],
            row_sums[2],
            other_sums[0],
            other_sums[1],
            other_sums[2],
            other_sums[3],
            other_sums[4],
            other_sums[5],
        ),
        ("rows", "cols"),
    )
    row_sums = summed[:3]
    other_sums = summed[3:]
    return (
        d_tokens,
        row_sums[0],
        row_sums[1],
        row_sums[2],
        other_sums[0],
        other_sums[1],
        other_sums[2],
        other_sums[3],
        other_sums[4],
        other_sums[5],
    )


def solution(mesh):
    in_specs = (
        P("rows", "cols", None),
        P("rows", "cols"),
        P("rows", "cols", None),
        P(),
        P(),
        P(),
        P(),
        P(),
        P(),
        P(),
        P(),
        P(),
    )
    out_specs = (P("rows", "cols", None), P(), P(), P(), P(), P(), P(), P(), P(), P())
    return jax.shard_map(shards, mesh=mesh, in_specs=in_specs, out_specs=out_specs, check_vma=False)
```

profile of v0, /device:TPU:0, one launch (start us, length us, event | category | flops | bytes accessed | tf_op | source)
XLA Modules:
  0.0 385.8 jit_solution(3843586543527307721)
XLA Ops:
  7.2 12.1 %all_to_all.134 = bf16[8,4,32]{2,1,0:T(4,128)(2,1)S(1)} all-to-all(bf16[8,4,32]{2,1,0:T(4,128)(2,1)} %bitcast.263), channel_id=1, replica_groups=mesh['rows'=4,'cols'=8] {'cols'}, dimensions={0} | all-to-all | bytes 4096 | tf_op jit(solution)/shard_map/all_to_all | solution.py:193
  19.3 3.6 all-to-all-start.1
  24.4 13.7 %all-to-all-done.1 = bf16[32,32,256]{2,1,0:T(8,128)(2,1)S(1)} async-done(((bf16[32,32,256]{2,1,0:T(8,128)(2,1)}), bf16[32,32,256]{2,1,0:T(8,128)(2,1)S(1)}, u32[]{:S(2)}, u32[]{:S(2)}) %all-to-all-start.1) | async-done | bytes 524320 | tf_op jit(solution)/shard_map/all_to_all | solution.py:192
  38.2 3.7 all-to-all-start.5
  46.3 4.7 %fusion.124 = (f32[4,4,256]{2,1,0:T(4,128)S(1)}, f32[4,4,256,256]{2,3,1,0:T(8,128)}) fusion(f32[4,256]{1,0:T(4,128)S(1)} %reshape.252, bf16[4,256,4,64]{1,3,2,0:T(8,128)(2,1)S(1)} %bitcast.249, bf16[4,256,4,64]{1,3,2,0:T(8,128)(2,1)} %bitcast.247), kind=kOutput, calls=%fused_computation.165 | convolution fusion | flops 138412288 | bytes 5263360 | tf_op jit(solution)/shard_map/while/body/eval_jaxpr/sub | solution.py:72
  51.0 2.7 convolution_convert_fusion.7
  56.1 3.5 all-to-all-start.3
  60.7 14.2 %all-to-all-done.3 = bf16[4,256,256]{2,0,1:T(4,128)(2,1)S(1)} async-done(((bf16[4,256,256]{2,0,1:T(4,128)(2,1)}), bf16[4,256,256]{2,0,1:T(4,128)(2,1)S(1)}, u32[]{:S(2)}, u32[]{:S(2)}) %all-to-all-start.3) | async-done | bytes 524320 | tf_op jit(solution)/shard_map/all_to_all | solution.py:199
  74.8 4.2 %all-to-all-start = ((bf16[32,32,256]{2,0,1:T(8,128)(2,1)}), bf16[32,32,256]{2,0,1:T(8,128)(2,1)S(1)}, u32[]{:S(2)}, u32[]{:S(2)}) async-start(bf16[32,32,256]{2,0,1:T(8,128)(2,1)} %copy.364), calls=%async_computation | async-start | bytes 1048576 | tf_op jit(solution)/shard_map/all_to_all | solution.py:206
  80.2 6.6 %all-to-all-done = bf16[32,32,256]{2,0,1:T(8,128)(2,1)S(1)} async-done(((bf16[32,32,256]{2,0,1:T(8,128)(2,1)}), bf16[32,32,256]{2,0,1:T(8,128)(2,1)S(1)}, u32[]{:S(2)}, u32[]{:S(2)}) %all-to-all-start) | async-done | bytes 524320 | tf_op jit(solution)/shard_map/all_to_all | solution.py:206
  86.9 3.7 all-to-all-start.4
  91.5 5.8 %all-to-all-done.4 = bf16[32,32,256]{2,0,1:T(8,128)(2,1)S(1)} async-done(((bf16[32,32,256]{2,0,1:T(8,128)(2,1)}), bf16[32,32,256]{2,0,1:T(8,128)(2,1)S(1)}, u32[]{:S(2)}, u32[]{:S(2)}) %all-to-all-start.4) | async-done | bytes 524320 | tf_op jit(solution)/shard_map/all_to_all | solution.py:198
  100.8 1.6 convolution_convert_fusion
  103.5 2.0 copy.387
  107.9 3.7 fusion.125
  111.6 2.0 convolution_convert_fusion.6
  115.3 2.8 multiply_convert_fusion
  118.2 3.2 fusion.10
  125.3 2.0 copy.392
  127.3 3.5 convolution_convert_fusion.5
  130.8 1.8 fusion.126
  132.6 5.2 %fusion.42 = bf16[8,4,64,128]{3,2,1,0:T(8,128)(2,1)} fusion(bf16[128,8,4,64]{0,3,2,1:T(8,128)(2,1)} %bitcast.252, f32[8,4,128,128]{2,3,1,0:T(8,128)} %fusion.126, f32[8,4,128,128]{2,3,1,0:T(8,128)} %get-tuple-element.127, f32[8,4,128]{2,1,0:T(4,128)S(1)} %get-tuple-element.126), kind=kOutput, calls=%fused_computation.49 | convolution fusion | flops 71045248 | bytes 5259264 | tf_op jit(solution)/shard_map/while/body/eval_jaxpr/shqk,kshd->qshd/dot_general | solution.py:10
  137.9 5.0 %fusion.45 = bf16[8,4,64,128]{3,2,1,0:T(8,128)(2,1)} fusion(bf16[128,8,4,64]{0,3,2,1:T(8,128)(2,1)S(1)} %bitcast.254, f32[8,4,128,128]{2,3,1,0:T(8,128)} %fusion.126, f32[8,4,128,128]{2,3,1,0:T(8,128)} %get-tuple-element.127, f32[8,4,128]{2,1,0:T(4,128)S(1)} %get-tuple-element.126), kind=kOutput, calls=%fused_computation.50 | convolution fusion | flops 71045248 | bytes 5259264 | tf_op jit(solution)/shard_map/while/body/eval_jaxpr/shqk,qshd->kshd/dot_general | solution.py:10
  144.1 2.2 copy.397
  146.4 2.0 copy.396
  148.4 3.2 multiply_reduce_fusion.2
  153.6 4.1 %all-to-all-start.6 = ((bf16[128,8,256]{2,1,0:T(8,128)(2,1)}), bf16[128,8,256]{2,1,0:T(8,128)(2,1)}, u32[]{:S(2)}, u32[]{:S(2)}) async-start(bf16[128,8,256]{2,1,0:T(8,128)(2,1)} %copy.399), calls=%async_computation.6 | async-start | bytes 1048576 | tf_op jit(solution)/shard_map/all_to_all | solution.py:221
  160.1 1.8 copy.416
  164.3 1.9 copy.454
  166.3 3.5 all-to-all-start.7
  170.1 2.3 convolution_multiply_fusion
  172.3 3.0 fusion.56
  175.3 2.0 fusion.38
  177.3 2.4 fusion.39
  179.7 5.3 %all-to-all-done.7 = bf16[32,32,256]{2,1,0:T(8,128)(2,1)S(1)} async-done(((bf16[32,32,256]{2,1,0:T(8,128)(2,1)}), bf16[32,32,256]{2,1,0:T(8,128)(2,1)S(1)}, u32[]{:S(2)}, u32[]{:S(2)}) %all-to-all-start.7) | async-done | bytes 524320 | tf_op jit(solution)/shard_map/all_to_all | solution.py:220
  185.4 3.8 convolution_convert_fusion.4
  189.3 2.7 fusion.127
  192.0 8.0 %fusion.48 = bf16[4,4,64,256]{3,2,1,0:T(8,128)(2,1)} fusion(bf16[4,256,4,64]{1,3,2,0:T(8,128)(2,1)S(1)} %bitcast.248, f32[4,4,256,256]{2,3,1,0:T(8,128)} %fusion.127, f32[4,4,256,256]{2,3,1,0:T(8,128)} %get-tuple-element.125, f32[4,4,256]{2,1,0:T(4,128)S(1)} %get-tuple-element.124), kind=kOutput, calls=%fused_computation.51 | convolution fusion | flops 141824256 | bytes 9453568 | tf_op jit(solution)/shard_map/while/body/eval_jaxpr/shqk,skhd->sqhd/dot_general | solution.py:10
  200.0 8.0 %fusion.51 = bf16[4,4,64,256]{3,2,1,0:T(8,128)(2,1)} fusion(bf16[4,256,4,64]{1,3,2,0:T(8,128)(2,1)S(1)} %bitcast.250, f32[4,4,256,256]{2,3,1,0:T(8,128)} %fusion.127, f32[4,4,256,256]{2,3,1,0:T(8,128)} %get-tuple-element.125, f32[4,4,256]{2,1,0:T(4,128)S(1)} %get-tuple-element.124), kind=kOutput, calls=%fused_computation.52 | convolution fusion | flops 141824256 | bytes 9453568 | tf_op jit(solution)/shard_map/while/body/eval_jaxpr/shqk,sqhd->skhd/dot_general | solution.py:10
  209.3 2.1 copy.406
  211.4 2.0 copy.405
  214.5 2.7 fusion.57
  221.9 3.5 all-to-all-start.8
  225.4 41.2 %all-reduce = (f32[256]{0:T(256)}, f32[256]{0:T(256)}, f32[256]{0:T(256)}) all-reduce(f32[256]{0:T(256)S(1)} %broadcast_multiply_fusion.11, f32[256]{0:T(256)S(1)} %broadcast_multiply_fusion.10, f32[256]{0:T(256)S(1)} %broadcast_multiply_fusion.9), channel_id=1, replica_groups=mesh['rows'=4,'cols'=8] {'rows','cols'}, use_global_device_ids=true, to_apply=%region_19.20 | all-reduce | flops 768 | bytes 6144 | tf_op jit(solution)/shard_map/psum | solution.py:232
  267.6 102.7 %all-reduce.4.cloned.1.call-done = (f32[256,768]{1,0:T(8,128)}, f32[256,256]{1,0:T(8,128)}, f32[256,768]{1,0:T(8,128)}, f32[256,256]{1,0:T(8,128)}, f32[256,1024]{1,0:T(8,128)}, /*index=5*/f32[1024,256]{1,0:T(8,128)}) async-done(((f32[256,768]{1,0:T(8,128)}, f32[256,256]{1,0:T(8,128)}, f32[256,768]{1,0:T(8,128)}, f32[256,256]{1,0:T(8,128)}, f32[256,1024]{1,0:T(8,128)}, /*index=5*/f32[1024,256]{1,0:T(8,128)}), ...) | async-done | bytes 4194320 | tf_op jit(solution)/shard_map/psum | solution.py:232
  370.2 2.2 copy.461
  372.5 1.7 copy.462
  374.2 2.1 copy.463
  (178 shorter events, 43.2 us)
Async XLA Ops:
  7.2 108.1 %copy-start = (bf16[256,1024]{1,0:T(8,128)(2,1)S(1)}, bf16[256,1024]{1,0:T(8,128)(2,1)}, u32[]{:S(2)}) copy-start(bf16[256,1024]{1,0:T(8,128)(2,1)} %param.22) | copy-start | bytes 1572868
  19.3 23.7 %copy-start.41 = (f32[256]{0:T(256)S(1)}, f32[256]{0:T(256)}, u32[]{:S(2)}) copy-start(f32[256]{0:T(256)} %param.15) | copy-start | bytes 3076
  19.3 18.9 %all-to-all-start.1 = ((bf16[32,32,256]{2,1,0:T(8,128)(2,1)}), bf16[32,32,256]{2,1,0:T(8,128)(2,1)S(1)}, u32[]{:S(2)}, u32[]{:S(2)}) async-start(bf16[32,32,256]{2,1,0:T(8,128)(2,1)} %param.12), calls=%async_computation.1 | async-start | bytes 1048576 | tf_op jit(solution)/shard_map/all_to_all | solution.py:192
  38.2 17.9 %all-to-all-start.5 = ((bf16[4,2,128]{2,1,0:T(2,128)(2,1)}), bf16[4,2,128]{2,1,0:T(2,128)(2,1)S(1)}, u32[]{:S(2)}, u32[]{:S(2)}) async-start(bf16[4,2,128]{2,1,0:T(2,128)(2,1)} %reshape.268), calls=%async_computation.5 | async-start | bytes 4096 | tf_op jit(solution)/shard_map/all_to_all | solution.py:207
  41.9 2.2 copy-start.36
  46.0 4.9 %copy-start.29 = (bf16[4,256,256]{1,2,0:T(8,128)(2,1)}, bf16[4,256,256]{1,2,0:T(8,128)(2,1)S(1)}, u32[]{:S(2)}) copy-start(bf16[4,256,256]{1,2,0:T(8,128)(2,1)S(1)} %copy.369) | copy-start | bytes 1572868
  46.2 4.7 %copy-start.8 = (bf16[4,256,256]{1,2,0:T(8,128)(2,1)}, bf16[4,256,256]{1,2,0:T(8,128)(2,1)S(1)}, u32[]{:S(2)}) copy-start(bf16[4,256,256]{1,2,0:T(8,128)(2,1)S(1)} %copy.368) | copy-start | bytes 1572868
  50.9 3.6 copy-start.26
  53.7 5.9 %copy-start.27 = (bf16[32,32,256]{2,1,0:T(8,128)(2,1)S(1)}, bf16[32,32,256]{2,1,0:T(8,128)(2,1)}, u32[]{:S(2)}) copy-start(bf16[32,32,256]{2,1,0:T(8,128)(2,1)} %param.14) | copy-start | bytes 1572868
  56.1 18.8 %all-to-all-start.3 = ((bf16[4,256,256]{2,0,1:T(4,128)(2,1)}), bf16[4,256,256]{2,0,1:T(4,128)(2,1)S(1)}, u32[]{:S(2)}, u32[]{:S(2)}) async-start(bf16[4,256,256]{2,0,1:T(4,128)(2,1)} %copy.374), calls=%async_computation.3 | async-start | bytes 1048576 | tf_op jit(solution)/shard_map/all_to_all | solution.py:199
  74.8 12.0 %all-to-all-start = ((bf16[32,32,256]{2,0,1:T(8,128)(2,1)}), bf16[32,32,256]{2,0,1:T(8,128)(2,1)S(1)}, u32[]{:S(2)}, u32[]{:S(2)}) async-start(bf16[32,32,256]{2,0,1:T(8,128)(2,1)} %copy.364), calls=%async_computation | async-start | bytes 1048576 | tf_op jit(solution)/shard_map/all_to_all | solution.py:206
  86.9 11.8 %copy-start.2 = (bf16[32,32,256]{2,0,1:T(8,128)(2,1)}, bf16[32,32,256]{2,0,1:T(8,128)(2,1)S(1)}, u32[]{:S(2)}) copy-start(bf16[32,32,256]{2,0,1:T(8,128)(2,1)S(1)} %all-to-all-done) | copy-start | bytes 1572868
  86.9 10.4 %all-to-all-start.4 = ((bf16[32,32,256]{2,0,1:T(8,128)(2,1)}), bf16[32,32,256]{2,0,1:T(8,128)(2,1)S(1)}, u32[]{:S(2)}, u32[]{:S(2)}) async-start(bf16[32,32,256]{2,0,1:T(8,128)(2,1)} %copy.377), calls=%async_computation.4 | async-start | bytes 1048576 | tf_op jit(solution)/shard_map/all_to_all | solution.py:198
  90.7 8.9 %copy-start.40 = (f32[256]{0:T(256)S(1)}, f32[256]{0:T(256)}, u32[]{:S(2)}) copy-start(f32[256]{0:T(256)} %param.18) | copy-start | bytes 3076
  107.9 5.8 %copy-start.20 = (bf16[128,8,256]{0,2,1:T(8,128)(2,1)}, bf16[128,8,256]{0,2,1:T(8,128)(2,1)S(1)}, u32[]{:S(2)}) copy-start(bf16[128,8,256]{0,2,1:T(8,128)(2,1)S(1)} %copy.385) | copy-start | bytes 1572868
  111.6 2.9 copy-start.25
  111.6 3.8 copy-start.39
  115.3 2.8 copy-start.12
  115.3 2.8 copy-start.44
  121.4 2.0 copy-start.13
  127.3 3.5 copy-start.21
  127.3 3.5 copy-start.22
  132.6 5.2 %copy-start.32 = (bf16[128,8,256]{0,2,1:T(8,128)(2,1)S(1)}, bf16[128,8,256]{0,2,1:T(8,128)(2,1)}, u32[]{:S(2)}) copy-start(bf16[128,8,256]{0,2,1:T(8,128)(2,1)} %copy.386) | copy-start | bytes 1572868
  144.1 4.3 %copy-start.31 = (bf16[128,8,256]{2,0,1:T(8,128)(2,1)}, bf16[128,8,256]{2,0,1:T(8,128)(2,1)S(1)}, u32[]{:S(2)}) copy-start(bf16[128,8,256]{2,0,1:T(8,128)(2,1)S(1)} %copy.398) | copy-start | bytes 1572868
  148.4 3.2 copy-start.5
  151.6 6.1 %copy-start.3 = (bf16[32,32,256]{2,0,1:T(8,128)(2,1)S(1)}, bf16[32,32,256]{2,0,1:T(8,128)(2,1)}, u32[]{:S(2)}) copy-start(bf16[32,32,256]{2,0,1:T(8,128)(2,1)} %copy-done.2) | copy-start | bytes 1572868
  152.5 6.3 %copy-start.11 = (bf16[4,4,64,256]{3,2,1,0:T(8,128)(2,1)S(1)}, bf16[4,4,64,256]{3,2,1,0:T(8,128)(2,1)}, u32[]{:S(2)}) copy-start(bf16[4,4,64,256]{3,2,1,0:T(8,128)(2,1)} %copy-done.10) | copy-start | bytes 1572868
  153.6 10.8 %all-to-all-start.6 = ((bf16[128,8,256]{2,1,0:T(8,128)(2,1)}), bf16[128,8,256]{2,1,0:T(8,128)(2,1)}, u32[]{:S(2)}, u32[]{:S(2)}) async-start(bf16[128,8,256]{2,1,0:T(8,128)(2,1)} %copy.399), calls=%async_computation.6 | async-start | bytes 1048576 | tf_op jit(solution)/shard_map/all_to_all | solution.py:221
  159.2 10.9 %copy-start.6 = (bf16[128,8,256]{2,0,1:T(8,128)(2,1)S(1)}, bf16[128,8,256]{2,0,1:T(8,128)(2,1)}, u32[]{:S(2)}) copy-start(bf16[128,8,256]{2,0,1:T(8,128)(2,1)} %copy-done.4) | copy-start | bytes 1572868
  163.5 8.9 %copy-start.18 = (bf16[128,8,256]{2,0,1:T(8,128)(2,1)S(1)}, bf16[128,8,256]{2,0,1:T(8,128)(2,1)}, u32[]{:S(2)}) copy-start(bf16[128,8,256]{2,0,1:T(8,128)(2,1)} %copy-done.17) | copy-start | bytes 1572868
  166.3 18.8 %all-to-all-start.7 = ((bf16[32,32,256]{2,1,0:T(8,128)(2,1)}), bf16[32,32,256]{2,1,0:T(8,128)(2,1)S(1)}, u32[]{:S(2)}, u32[]{:S(2)}) async-start(bf16[32,32,256]{2,1,0:T(8,128)(2,1)} %bitcast.239), calls=%async_computation.7 | async-start | bytes 1048576 | tf_op jit(solution)/shard_map/all_to_all | solution.py:220
  169.8 200.5 %all-reduce.4.cloned.1.call-start = ((), (), s32[]{:S(2)}) async-start(), calls=%async_computation.9 | async-start | bytes 8388608 | tf_op jit(solution)/shard_map/psum | solution.py:232
  172.3 3.0 copy-start.14
  175.3 2.0 copy-start.33
  175.3 2.0 copy-start.45
  185.4 3.8 copy-start.9
  189.3 2.7 copy-start.28
  192.0 8.0 %copy-start.30 = (bf16[4,256,256]{1,2,0:T(8,128)(2,1)S(1)}, bf16[4,256,256]{1,2,0:T(8,128)(2,1)}, u32[]{:S(2)}) copy-start(bf16[4,256,256]{1,2,0:T(8,128)(2,1)} %copy-done.29) | copy-start | bytes 1572868
  208.0 5.5 %copy-start.19 = (bf16[32,8,4,256]{3,1,2,0:T(8,128)(2,1)S(1)}, bf16[32,8,4,256]{3,1,2,0:T(8,128)(2,1)}, u32[]{:S(2)}) copy-start(bf16[32,8,4,256]{3,1,2,0:T(8,128)(2,1)} %copy.437) | copy-start | bytes 1572868
  208.0 6.5 %copy-start.16 = (bf16[4,256,256]{2,1,0:T(8,128)(2,1)S(1)}, bf16[4,256,256]{2,1,0:T(8,128)(2,1)}, u32[]{:S(2)}) copy-start(bf16[4,256,256]{2,1,0:T(8,128)(2,1)} %copy-done.15) | copy-start | bytes 1572868
  217.2 1.3 copy-start.37
  219.8 5.6 %copy-start.42 = (f32[256]{0:T(256)S(1)}, f32[256]{0:T(256)}, u32[]{:S(2)}) copy-start(f32[256]{0:T(256)} %get-tuple-element.73) | copy-start | bytes 3076
  219.8 5.6 %copy-start.43 = (f32[256]{0:T(256)S(1)}, f32[256]{0:T(256)}, u32[]{:S(2)}) copy-start(f32[256]{0:T(256)} %get-tuple-element.84) | copy-start | bytes 3076
  221.9 44.8 %all-to-all-start.8 = ((bf16[4,256,256]{2,0,1:T(4,128)(2,1)}), bf16[4,256,256]{2,0,1:T(4,128)(2,1)S(1)}, u32[]{:S(2)}, u32[]{:S(2)}) async-start(bf16[4,256,256]{2,0,1:T(4,128)(2,1)} %copy.409), calls=%async_computation.8 | async-start | bytes 1048576 | tf_op jit(solution)/shard_map/all_to_all | solution.py:230
  370.2 6.0 %copy-start.38 = (f32[256,256]{1,0:T(8,128)S(1)}, f32[256,256]{1,0:T(8,128)}, u32[]{:S(2)}) copy-start(f32[256,256]{1,0:T(8,128)} %get-tuple-element.143) | copy-start | bytes 786436
  370.2 6.7 %copy-start.24 = (f32[256,1024]{1,0:T(8,128)S(1)}, f32[256,1024]{1,0:T(8,128)}, u32[]{:S(2)}) copy-start(f32[256,1024]{1,0:T(8,128)} %get-tuple-element.145) | copy-start | bytes 3145732
  370.2 7.7 %copy-start.23 = (f32[1024,256]{1,0:T(8,128)S(1)}, f32[1024,256]{1,0:T(8,128)}, u32[]{:S(2)}) copy-start(f32[1024,256]{1,0:T(8,128)} %get-tuple-element.146) | copy-start | bytes 3145732
  372.5 6.4 %copy-start.1 = (bf16[256,1024]{1,0:T(8,128)(2,1)S(1)}, bf16[256,1024]{1,0:T(8,128)(2,1)}, u32[]{:S(2)}) copy-start(bf16[256,1024]{1,0:T(8,128)(2,1)} %param.22) | copy-start | bytes 1572868
  (7 other events, 6.3 us)
Sparse Core Ops, SparseCore 0:
  217.3 152.8 all-reduce.3
where the time goes:
time: 387 us; the launch traced here: 386 us
  waiting for transfers between devices  149 us (39%)
  matrix products  80.4 us (21%)
  blocking collectives  53.3 us (14%)
  local copies, waits for them, and re-layouts  52.3 us (14%)
  starting transfers between devices  30.1 us (8%)
  between operations  14.7 us (4%)
  other arithmetic  5.81 us (2%)
    psum x1, waiting for transfers between devices, shards(): lax.psum((row_sums[0], row_sums[1], row_sums[2], other_sums[0], other_sum...  103 us
    dot_general x10, matrix products, product(): jnp.einsum(spec_text, left_op, right_op, preferred_element_type=jnp.float32)  42.8 us
    psum x1, blocking collectives, shards(): lax.psum((row_sums[0], row_sums[1], row_sums[2], other_sums[0], other_sum...  41.2 us
    unnamed x104, local copies, waits for them, and re-layouts  17.6 us
    all_to_all x1, waiting for transfers between devices, shards(): lax.all_to_all(after_rows, 'cols', split_axis=1, concat_axis=0, tiled=True)  14.2 us
    all_to_all x1, waiting for transfers between devices, shards(): lax.all_to_all(tokens, 'cols', split_axis=0, concat_axis=1, tiled=True)  13.7 us
    dot_general x6, matrix products, over_cells(): lax.dot_general(left_flat, right_flat, (((0,), (0,)), ((), ())), preferre...  13.3 us
    all_to_all x1, blocking collectives, shards(): lax.all_to_all(key_bias, 'cols', split_axis=0, concat_axis=1, tiled=True)  12.1 us
  transfers between devices with their start and end apart: 9, of which 7 were waited for; matrix products, arithmetic and copies ran while one was open for 10% of the time, Pallas kernels for 0%

commit v1 on v0

--- a/solution.py
+++ b/solution.py
@@ -4,6 +4,12 @@
 from jax.sharding import PartitionSpec as P
 
 HEADS = 4
+
+
+def exchange_blocks(block, axis, split, join):
+    cells = jnp.split(block, lax.axis_size(axis), axis=split)
+    incoming = lax.all_to_all(jnp.stack(cells), axis, 0, 0)
+    return jnp.concatenate(incoming, axis=join)
 
 
 def product(spec_text, left_op, right_op):
@@ -190,7 +196,7 @@
 ):
     row_cells, row_bias = (
         lax.all_to_all(tokens, "cols", split_axis=0, concat_axis=1, tiled=True),
-        lax.all_to_all(key_bias, "cols", split_axis=0, concat_axis=1, tiled=True),
+        exchange_blocks(key_bias, "cols", 0, 1),
     )
     after_rows, row_saved = attention_forward(
         row_cells, row_bias, gain_row, w_qkv_row, w_out_row, HEADS, 1

time: 387 us -> 393 us (1.016)
  local copies, waits for them, and re-layouts: 52.3 us -> 58.2 us
    unnamed x104 -> x111, local copies, waits for them, and re-layouts: 17.6 us -> 21.7 us
  transfers between devices with their start and end apart: 9 -> 9, of which waited for: 7 -> 7; matrix products, arithmetic and copies ran while one was open for 10% -> 9% of each run, Pallas kernels for 0% -> 0%
where the time goes in v1:
time: 393 us; the launch traced here: 391 us
  waiting for transfers between devices  149 us (38%)
  matrix products  80.6 us (21%)
  local copies, waits for them, and re-layouts  58.2 us (15%)
  blocking collectives  53 us (13%)
  starting transfers between devices  30.1 us (8%)
  between operations  14.7 us (4%)
  other arithmetic  5.81 us (1%)
    psum x1, waiting for transfers between devices, shards(): lax.psum((row_sums[0], row_sums[1], row_sums[2], other_sums[0], other_sum...  103 us
    dot_general x10, matrix products, product(): jnp.einsum(spec_text, left_op, right_op, preferred_element_type=jnp.float32)  42.9 us
    psum x1, blocking collectives, shards(): lax.psum((row_sums[0], row_sums[1], row_sums[2], other_sums[0], other_sum...  41.3 us
    unnamed x111, local copies, waits for them, and re-layouts  21.7 us
    all_to_all x1, waiting for transfers between devices, shards(): lax.all_to_all(after_rows, 'cols', split_axis=1, concat_axis=0, tiled=True)  14.2 us
    all_to_all x1, waiting for transfers between devices, shards(): lax.all_to_all(tokens, 'cols', split_axis=0, concat_axis=1, tiled=True)  13.7 us
    dot_general x6, matrix products, over_cells(): lax.dot_general(left_flat, right_flat, (((0,), (0,)), ((), ())), preferre...  13.3 us
    all_to_all x1, blocking collectives, exchange_blocks(): incoming = lax.all_to_all(jnp.stack(cells), axis, 0, 0)  11.7 us
  transfers between devices with their start and end apart: 9, of which 7 were waited for; matrix products, arithmetic and copies ran while one was open for 9% of the time, Pallas kernels for 0%

profile of v1, /device:TPU:0, one launch (start us, length us, event | category | flops | bytes accessed | tf_op | source)
XLA Modules:
  0.0 391.4 jit_solution(10200569974729738327)
XLA Ops:
  12.8 11.7 %all_to_all.126 = bf16[8,4,32]{2,1,0:T(4,128)(2,1)S(1)} all-to-all(bf16[8,4,32]{2,1,0:T(4,128)(2,1)S(1)} %constant_dynamic-update-slice_fusion), channel_id=1, replica_groups=mesh['rows'=4,'cols'=8] {'cols'}, dimensions={0} | all-to-all | bytes 4096 | tf_op jit(solution)/shard_map/all_to_all | solution.py:11
  24.5 3.6 all-to-all-start.1
  29.7 13.7 %all-to-all-done.1 = bf16[32,32,256]{2,1,0:T(8,128)(2,1)S(1)} async-done(((bf16[32,32,256]{2,1,0:T(8,128)(2,1)}), bf16[32,32,256]{2,1,0:T(8,128)(2,1)S(1)}, u32[]{:S(2)}, u32[]{:S(2)}) %all-to-all-start.1) | async-done | bytes 524320 | tf_op jit(solution)/shard_map/all_to_all | solution.py:198
  43.4 3.7 all-to-all-start.5
  51.5 4.7 %fusion.124 = (f32[4,4,256]{2,1,0:T(4,128)S(1)}, f32[4,4,256,256]{2,3,1,0:T(8,128)}) fusion(f32[4,256]{1,0:T(4,128)S(1)} %reshape.251, bf16[4,256,4,64]{1,3,2,0:T(8,128)(2,1)S(1)} %bitcast.264, bf16[4,256,4,64]{1,3,2,0:T(8,128)(2,1)} %bitcast.262), kind=kOutput, calls=%fused_computation.173 | convolution fusion | flops 138412288 | bytes 5263360 | tf_op jit(solution)/shard_map/while/body/eval_jaxpr/sub | solution.py:78
  56.2 2.7 convolution_convert_fusion.7
  61.3 3.5 all-to-all-start.3
  65.9 14.2 %all-to-all-done.3 = bf16[4,256,256]{2,0,1:T(4,128)(2,1)S(1)} async-done(((bf16[4,256,256]{2,0,1:T(4,128)(2,1)}), bf16[4,256,256]{2,0,1:T(4,128)(2,1)S(1)}, u32[]{:S(2)}, u32[]{:S(2)}) %all-to-all-start.3) | async-done | bytes 524320 | tf_op jit(solution)/shard_map/all_to_all | solution.py:205
  80.1 4.2 %all-to-all-start = ((bf16[32,32,256]{2,0,1:T(8,128)(2,1)}), bf16[32,32,256]{2,0,1:T(8,128)(2,1)S(1)}, u32[]{:S(2)}, u32[]{:S(2)}) async-start(bf16[32,32,256]{2,0,1:T(8,128)(2,1)} %copy.363), calls=%async_computation | async-start | bytes 1048576 | tf_op jit(solution)/shard_map/all_to_all | solution.py:212
  85.5 6.6 %all-to-all-done = bf16[32,32,256]{2,0,1:T(8,128)(2,1)S(1)} async-done(((bf16[32,32,256]{2,0,1:T(8,128)(2,1)}), bf16[32,32,256]{2,0,1:T(8,128)(2,1)S(1)}, u32[]{:S(2)}, u32[]{:S(2)}) %all-to-all-start) | async-done | bytes 524320 | tf_op jit(solution)/shard_map/all_to_all | solution.py:212
  92.1 3.7 all-to-all-start.4
  96.8 5.7 %all-to-all-done.4 = bf16[32,32,256]{2,0,1:T(8,128)(2,1)S(1)} async-done(((bf16[32,32,256]{2,0,1:T(8,128)(2,1)}), bf16[32,32,256]{2,0,1:T(8,128)(2,1)S(1)}, u32[]{:S(2)}, u32[]{:S(2)}) %all-to-all-start.4) | async-done | bytes 524320 | tf_op jit(solution)/shard_map/all_to_all | solution.py:204
  105.2 1.8 convolution_convert_fusion
  108.2 2.0 copy.386
  110.2 2.0 copy.385
  113.6 3.7 fusion.125
  117.3 2.0 convolution_convert_fusion.6
  121.0 2.8 multiply_convert_fusion
  123.9 3.2 fusion.10
  131.0 2.0 copy.391
  133.0 3.5 convolution_convert_fusion.5
  136.5 1.8 fusion.126
  138.3 5.2 %fusion.42 = bf16[8,4,64,128]{3,2,1,0:T(8,128)(2,1)} fusion(bf16[128,8,4,64]{0,3,2,1:T(8,128)(2,1)} %bitcast.267, f32[8,4,128,128]{2,3,1,0:T(8,128)} %fusion.126, f32[8,4,128,128]{2,3,1,0:T(8,128)} %get-tuple-element.127, f32[8,4,128]{2,1,0:T(4,128)S(1)} %get-tuple-element.126), kind=kOutput, calls=%fused_computation.49 | convolution fusion | flops 71045248 | bytes 5259264 | tf_op jit(solution)/shard_map/while/body/eval_jaxpr/shqk,kshd->qshd/dot_general | solution.py:16
  143.6 5.0 %fusion.45 = bf16[8,4,64,128]{3,2,1,0:T(8,128)(2,1)} fusion(bf16[128,8,4,64]{0,3,2,1:T(8,128)(2,1)S(1)} %bitcast.269, f32[8,4,128,128]{2,3,1,0:T(8,128)} %fusion.126, f32[8,4,128,128]{2,3,1,0:T(8,128)} %get-tuple-element.127, f32[8,4,128]{2,1,0:T(4,128)S(1)} %get-tuple-element.126), kind=kOutput, calls=%fused_computation.50 | convolution fusion | flops 71045248 | bytes 5259264 | tf_op jit(solution)/shard_map/while/body/eval_jaxpr/shqk,qshd->kshd/dot_general | solution.py:16
  149.8 2.2 copy.396
  152.1 2.0 copy.395
  154.1 3.2 multiply_reduce_fusion.2
  159.2 4.1 %all-to-all-start.6 = ((bf16[128,8,256]{2,1,0:T(8,128)(2,1)}), bf16[128,8,256]{2,1,0:T(8,128)(2,1)}, u32[]{:S(2)}, u32[]{:S(2)}) async-start(bf16[128,8,256]{2,1,0:T(8,128)(2,1)} %copy.398), calls=%async_computation.6 | async-start | bytes 1048576 | tf_op jit(solution)/shard_map/all_to_all | solution.py:227
  165.9 1.8 copy.415
  170.0 1.9 copy.453
  172.0 3.5 all-to-all-start.7
  175.8 2.3 convolution_multiply_fusion
  178.0 3.0 fusion.56
  181.0 2.0 fusion.38
  183.0 2.4 fusion.39
  185.4 5.3 %all-to-all-done.7 = bf16[32,32,256]{2,1,0:T(8,128)(2,1)S(1)} async-done(((bf16[32,32,256]{2,1,0:T(8,128)(2,1)}), bf16[32,32,256]{2,1,0:T(8,128)(2,1)S(1)}, u32[]{:S(2)}, u32[]{:S(2)}) %all-to-all-start.7) | async-done | bytes 524320 | tf_op jit(solution)/shard_map/all_to_all | solution.py:226
  191.1 3.8 convolution_convert_fusion.4
  195.0 2.7 fusion.127
  197.7 8.0 %fusion.48 = bf16[4,4,64,256]{3,2,1,0:T(8,128)(2,1)} fusion(bf16[4,256,4,64]{1,3,2,0:T(8,128)(2,1)S(1)} %bitcast.263, f32[4,4,256,256]{2,3,1,0:T(8,128)} %fusion.127, f32[4,4,256,256]{2,3,1,0:T(8,128)} %get-tuple-element.125, f32[4,4,256]{2,1,0:T(4,128)S(1)} %get-tuple-element.124), kind=kOutput, calls=%fused_computation.51 | convolution fusion | flops 141824256 | bytes 9453568 | tf_op jit(solution)/shard_map/while/body/eval_jaxpr/shqk,skhd->sqhd/dot_general | solution.py:16
  205.7 8.0 %fusion.51 = bf16[4,4,64,256]{3,2,1,0:T(8,128)(2,1)} fusion(bf16[4,256,4,64]{1,3,2,0:T(8,128)(2,1)S(1)} %bitcast.265, f32[4,4,256,256]{2,3,1,0:T(8,128)} %fusion.127, f32[4,4,256,256]{2,3,1,0:T(8,128)} %get-tuple-element.125, f32[4,4,256]{2,1,0:T(4,128)S(1)} %get-tuple-element.124), kind=kOutput, calls=%fused_computation.52 | convolution fusion | flops 141824256 | bytes 9453568 | tf_op jit(solution)/shard_map/while/body/eval_jaxpr/shqk,sqhd->skhd/dot_general | solution.py:16
  215.0 2.1 copy.405
  217.1 2.0 copy.404
  220.2 2.7 fusion.57
  227.6 3.5 all-to-all-start.8
  231.1 41.3 %all-reduce = (f32[256]{0:T(256)}, f32[256]{0:T(256)}, f32[256]{0:T(256)}) all-reduce(f32[256]{0:T(256)S(1)} %broadcast_multiply_fusion.11, f32[256]{0:T(256)S(1)} %broadcast_multiply_fusion.10, f32[256]{0:T(256)S(1)} %broadcast_multiply_fusion.9), channel_id=1, replica_groups=mesh['rows'=4,'cols'=8] {'rows','cols'}, use_global_device_ids=true, to_apply=%region_19.20 | all-reduce | flops 768 | bytes 6144 | tf_op jit(solution)/shard_map/psum | solution.py:238
  273.3 102.6 %all-reduce.4.cloned.1.call-done = (f32[256,768]{1,0:T(8,128)}, f32[256,256]{1,0:T(8,128)}, f32[256,768]{1,0:T(8,128)}, f32[256,256]{1,0:T(8,128)}, f32[256,1024]{1,0:T(8,128)}, /*index=5*/f32[1024,256]{1,0:T(8,128)}) async-done(((f32[256,768]{1,0:T(8,128)}, f32[256,256]{1,0:T(8,128)}, f32[256,768]{1,0:T(8,128)}, f32[256,256]{1,0:T(8,128)}, f32[256,1024]{1,0:T(8,128)}, /*index=5*/f32[1024,256]{1,0:T(8,128)}), ...) | async-done | bytes 4194320 | tf_op jit(solution)/shard_map/psum | solution.py:238
  375.9 2.2 copy.467
  379.9 2.1 copy.469
  (186 shorter events, 48.7 us)
Async XLA Ops:
  7.2 113.8 %copy-start = (bf16[256,1024]{1,0:T(8,128)(2,1)S(1)}, bf16[256,1024]{1,0:T(8,128)(2,1)}, u32[]{:S(2)}) copy-start(bf16[256,1024]{1,0:T(8,128)(2,1)} %param.22) | copy-start | bytes 1572868
  24.5 23.7 %copy-start.41 = (f32[256]{0:T(256)S(1)}, f32[256]{0:T(256)}, u32[]{:S(2)}) copy-start(f32[256]{0:T(256)} %param.15) | copy-start | bytes 3076
  24.5 18.9 %all-to-all-start.1 = ((bf16[32,32,256]{2,1,0:T(8,128)(2,1)}), bf16[32,32,256]{2,1,0:T(8,128)(2,1)S(1)}, u32[]{:S(2)}, u32[]{:S(2)}) async-start(bf16[32,32,256]{2,1,0:T(8,128)(2,1)} %param.12), calls=%async_computation.1 | async-start | bytes 1048576 | tf_op jit(solution)/shard_map/all_to_all | solution.py:198
  43.4 17.9 %all-to-all-start.5 = ((bf16[4,2,128]{2,1,0:T(2,128)(2,1)}), bf16[4,2,128]{2,1,0:T(2,128)(2,1)S(1)}, u32[]{:S(2)}, u32[]{:S(2)}) async-start(bf16[4,2,128]{2,1,0:T(2,128)(2,1)} %reshape.267), calls=%async_computation.5 | async-start | bytes 4096 | tf_op jit(solution)/shard_map/all_to_all | solution.py:213
  47.1 2.2 copy-start.36
  51.3 4.9 %copy-start.29 = (bf16[4,256,256]{1,2,0:T(8,128)(2,1)}, bf16[4,256,256]{1,2,0:T(8,128)(2,1)S(1)}, u32[]{:S(2)}) copy-start(bf16[4,256,256]{1,2,0:T(8,128)(2,1)S(1)} %copy.368) | copy-start | bytes 1572868
  51.5 4.7 %copy-start.8 = (bf16[4,256,256]{1,2,0:T(8,128)(2,1)}, bf16[4,256,256]{1,2,0:T(8,128)(2,1)S(1)}, u32[]{:S(2)}) copy-start(bf16[4,256,256]{1,2,0:T(8,128)(2,1)S(1)} %copy.367) | copy-start | bytes 1572868
  56.2 3.6 copy-start.26
  58.9 5.9 %copy-start.27 = (bf16[32,32,256]{2,1,0:T(8,128)(2,1)S(1)}, bf16[32,32,256]{2,1,0:T(8,128)(2,1)}, u32[]{:S(2)}) copy-start(bf16[32,32,256]{2,1,0:T(8,128)(2,1)} %param.14) | copy-start | bytes 1572868
  61.3 18.8 %all-to-all-start.3 = ((bf16[4,256,256]{2,0,1:T(4,128)(2,1)}), bf16[4,256,256]{2,0,1:T(4,128)(2,1)S(1)}, u32[]{:S(2)}, u32[]{:S(2)}) async-start(bf16[4,256,256]{2,0,1:T(4,128)(2,1)} %copy.373), calls=%async_computation.3 | async-start | bytes 1048576 | tf_op jit(solution)/shard_map/all_to_all | solution.py:205
  80.1 12.0 %all-to-all-start = ((bf16[32,32,256]{2,0,1:T(8,128)(2,1)}), bf16[32,32,256]{2,0,1:T(8,128)(2,1)S(1)}, u32[]{:S(2)}, u32[]{:S(2)}) async-start(bf16[32,32,256]{2,0,1:T(8,128)(2,1)} %copy.363), calls=%async_computation | async-start | bytes 1048576 | tf_op jit(solution)/shard_map/all_to_all | solution.py:212
  92.1 11.8 %copy-start.2 = (bf16[32,32,256]{2,0,1:T(8,128)(2,1)}, bf16[32,32,256]{2,0,1:T(8,128)(2,1)S(1)}, u32[]{:S(2)}) copy-start(bf16[32,32,256]{2,0,1:T(8,128)(2,1)S(1)} %all-to-all-done) | copy-start | bytes 1572868
  92.1 10.4 %all-to-all-start.4 = ((bf16[32,32,256]{2,0,1:T(8,128)(2,1)}), bf16[32,32,256]{2,0,1:T(8,128)(2,1)S(1)}, u32[]{:S(2)}, u32[]{:S(2)}) async-start(bf16[32,32,256]{2,0,1:T(8,128)(2,1)} %copy.376), calls=%async_computation.4 | async-start | bytes 1048576 | tf_op jit(solution)/shard_map/all_to_all | solution.py:204
  95.9 8.9 %copy-start.40 = (f32[256]{0:T(256)S(1)}, f32[256]{0:T(256)}, u32[]{:S(2)}) copy-start(f32[256]{0:T(256)} %param.18) | copy-start | bytes 3076
  105.2 5.0 %copy-start.17 = (bf16[128,8,256]{2,0,1:T(8,128)(2,1)}, bf16[128,8,256]{2,0,1:T(8,128)(2,1)S(1)}, u32[]{:S(2)}) copy-start(bf16[128,8,256]{2,0,1:T(8,128)(2,1)S(1)} %multiply_convert_fusion.3) | copy-start | bytes 1572868
  113.6 5.8 %copy-start.20 = (bf16[128,8,256]{0,2,1:T(8,128)(2,1)}, bf16[128,8,256]{0,2,1:T(8,128)(2,1)S(1)}, u32[]{:S(2)}) copy-start(bf16[128,8,256]{0,2,1:T(8,128)(2,1)S(1)} %copy.384) | copy-start | bytes 1572868
  117.3 2.9 copy-start.25
  117.3 3.7 copy-start.39
  121.0 2.8 copy-start.12
  121.0 2.8 copy-start.44
  127.1 2.0 copy-start.13
  133.0 3.5 copy-start.21
  133.0 3.5 copy-start.22
  138.3 5.2 %copy-start.32 = (bf16[128,8,256]{0,2,1:T(8,128)(2,1)S(1)}, bf16[128,8,256]{0,2,1:T(8,128)(2,1)}, u32[]{:S(2)}) copy-start(bf16[128,8,256]{0,2,1:T(8,128)(2,1)} %copy.385) | copy-start | bytes 1572868
  149.8 4.3 %copy-start.31 = (bf16[128,8,256]{2,0,1:T(8,128)(2,1)}, bf16[128,8,256]{2,0,1:T(8,128)(2,1)S(1)}, u32[]{:S(2)}) copy-start(bf16[128,8,256]{2,0,1:T(8,128)(2,1)S(1)} %copy.397) | copy-start | bytes 1572868
  154.1 3.2 copy-start.5
  157.3 6.1 %copy-start.3 = (bf16[32,32,256]{2,0,1:T(8,128)(2,1)S(1)}, bf16[32,32,256]{2,0,1:T(8,128)(2,1)}, u32[]{:S(2)}) copy-start(bf16[32,32,256]{2,0,1:T(8,128)(2,1)} %copy-done.2) | copy-start | bytes 1572868
  158.2 6.4 %copy-start.11 = (bf16[4,4,64,256]{3,2,1,0:T(8,128)(2,1)S(1)}, bf16[4,4,64,256]{3,2,1,0:T(8,128)(2,1)}, u32[]{:S(2)}) copy-start(bf16[4,4,64,256]{3,2,1,0:T(8,128)(2,1)} %copy-done.10) | copy-start | bytes 1572868
  159.2 10.8 %all-to-all-start.6 = ((bf16[128,8,256]{2,1,0:T(8,128)(2,1)}), bf16[128,8,256]{2,1,0:T(8,128)(2,1)}, u32[]{:S(2)}, u32[]{:S(2)}) async-start(bf16[128,8,256]{2,1,0:T(8,128)(2,1)} %copy.398), calls=%async_computation.6 | async-start | bytes 1048576 | tf_op jit(solution)/shard_map/all_to_all | solution.py:227
  164.9 10.8 %copy-start.6 = (bf16[128,8,256]{2,0,1:T(8,128)(2,1)S(1)}, bf16[128,8,256]{2,0,1:T(8,128)(2,1)}, u32[]{:S(2)}) copy-start(bf16[128,8,256]{2,0,1:T(8,128)(2,1)} %copy-done.4) | copy-start | bytes 1572868
  169.2 8.9 %copy-start.18 = (bf16[128,8,256]{2,0,1:T(8,128)(2,1)S(1)}, bf16[128,8,256]{2,0,1:T(8,128)(2,1)}, u32[]{:S(2)}) copy-start(bf16[128,8,256]{2,0,1:T(8,128)(2,1)} %copy-done.17) | copy-start | bytes 1572868
  172.0 18.8 %all-to-all-start.7 = ((bf16[32,32,256]{2,1,0:T(8,128)(2,1)}), bf16[32,32,256]{2,1,0:T(8,128)(2,1)S(1)}, u32[]{:S(2)}, u32[]{:S(2)}) async-start(bf16[32,32,256]{2,1,0:T(8,128)(2,1)} %bitcast.254), calls=%async_computation.7 | async-start | bytes 1048576 | tf_op jit(solution)/shard_map/all_to_all | solution.py:226
  175.5 200.5 %all-reduce.4.cloned.1.call-start = ((), (), s32[]{:S(2)}) async-start(), calls=%async_computation.9 | async-start | bytes 8388608 | tf_op jit(solution)/shard_map/psum | solution.py:238
  178.0 3.0 copy-start.14
  181.0 2.0 copy-start.33
  181.0 2.0 copy-start.45
  191.1 3.8 copy-start.9
  195.0 2.7 copy-start.28
  197.7 8.0 %copy-start.30 = (bf16[4,256,256]{1,2,0:T(8,128)(2,1)S(1)}, bf16[4,256,256]{1,2,0:T(8,128)(2,1)}, u32[]{:S(2)}) copy-start(bf16[4,256,256]{1,2,0:T(8,128)(2,1)} %copy-done.29) | copy-start | bytes 1572868
  213.7 5.5 %copy-start.19 = (bf16[32,8,4,256]{3,1,2,0:T(8,128)(2,1)S(1)}, bf16[32,8,4,256]{3,1,2,0:T(8,128)(2,1)}, u32[]{:S(2)}) copy-start(bf16[32,8,4,256]{3,1,2,0:T(8,128)(2,1)} %copy.436) | copy-start | bytes 1572868
  213.7 6.5 %copy-start.16 = (bf16[4,256,256]{2,1,0:T(8,128)(2,1)S(1)}, bf16[4,256,256]{2,1,0:T(8,128)(2,1)}, u32[]{:S(2)}) copy-start(bf16[4,256,256]{2,1,0:T(8,128)(2,1)} %copy-done.15) | copy-start | bytes 1572868
  225.5 5.6 %copy-start.42 = (f32[256]{0:T(256)S(1)}, f32[256]{0:T(256)}, u32[]{:S(2)}) copy-start(f32[256]{0:T(256)} %get-tuple-element.73) | copy-start | bytes 3076
  225.5 5.6 %copy-start.43 = (f32[256]{0:T(256)S(1)}, f32[256]{0:T(256)}, u32[]{:S(2)}) copy-start(f32[256]{0:T(256)} %get-tuple-element.84) | copy-start | bytes 3076
  227.6 44.8 %all-to-all-start.8 = ((bf16[4,256,256]{2,0,1:T(4,128)(2,1)}), bf16[4,256,256]{2,0,1:T(4,128)(2,1)S(1)}, u32[]{:S(2)}, u32[]{:S(2)}) async-start(bf16[4,256,256]{2,0,1:T(4,128)(2,1)} %copy.408), calls=%async_computation.8 | async-start | bytes 1048576 | tf_op jit(solution)/shard_map/all_to_all | solution.py:236
  375.9 6.0 %copy-start.38 = (f32[256,256]{1,0:T(8,128)S(1)}, f32[256,256]{1,0:T(8,128)}, u32[]{:S(2)}) copy-start(f32[256,256]{1,0:T(8,128)} %get-tuple-element.143) | copy-start | bytes 786436
  375.9 6.7 %copy-start.24 = (f32[256,1024]{1,0:T(8,128)S(1)}, f32[256,1024]{1,0:T(8,128)}, u32[]{:S(2)}) copy-start(f32[256,1024]{1,0:T(8,128)} %get-tuple-element.145) | copy-start | bytes 3145732
  375.9 7.7 %copy-start.23 = (f32[1024,256]{1,0:T(8,128)S(1)}, f32[1024,256]{1,0:T(8,128)}, u32[]{:S(2)}) copy-start(f32[1024,256]{1,0:T(8,128)} %get-tuple-element.146) | copy-start | bytes 3145732
  378.1 6.4 %copy-start.1 = (bf16[256,1024]{1,0:T(8,128)(2,1)S(1)}, bf16[256,1024]{1,0:T(8,128)(2,1)}, u32[]{:S(2)}) copy-start(bf16[256,1024]{1,0:T(8,128)(2,1)} %param.22) | copy-start | bytes 1572868
  (7 other events, 6.8 us)
Sparse Core Ops, SparseCore 0:
  223.0 152.8 all-reduce.3
